TPU v7x, 32 devices: a whole 2x2x4 slice. The times are simulated.
32 devices in a mesh: row: 8 (over z, x), col: 4 (over y, core).
Axes of the slice: x: 2, y: 2, z: 4, core: 2. Of those that a mesh axis runs over, the one named last changes fastest.
Arguments:
- krylov_block: bfloat16 [64, 16384], P(None, ('row', 'col')), may hold values from -54 to 54
- degree: int32 [16384], P(('row', 'col')), may hold values from 16 to 64
- tile_values: bfloat16 [256, 4, 64, 512], P('row', 'col'), may hold values from -6 to 6
- tile_column: int32 [256, 4, 8], P('row', 'col'), may hold values from 0 to 63
- tile_live: int32 [256, 4, 8], P('row', 'col'), may hold values 0 or 1
Outputs:
- orthonormal: float32 [64, 16384], P(None, ('row', 'col'))
- quotient: float32 [64, 64], replicated
All inputs are finite; a program needn't handle non-finite values. No bound on the sum of `tile_live` on one device may be relied on, other than what follows from the above.
Results may differ from a plain program's by a relative error of at most 0.0032.
Values may be sent and summed in bfloat16 or wider, within the bound.
No kernel may reach another device: no remote copies, remote signals or barrier semaphores. Data moves between devices by JAX's collectives and lax.ppermute only.
A program may use at most 128 MiB of HBM per device.

v0:
```python
import math
import jax
import jax.numpy as jnp
from jax import lax
from jax.sharding import PartitionSpec as P


def gram_of(left, right):
    return lax.dot_general(
        left,
        right,
        (((1,), (1,)), ((), ())),
        precision=lax.Precision.HIGHEST,
        preferred_element_type=jnp.float32,
    )


def on_device(krylov_block, degree, tile_values, tile_column, tile_live):
    vectors = krylov_block.shape[0]
    owned_rows = krylov_block.shape[1]
    block_rows = tile_values.shape[0]
    height = tile_values.shape[2]
    slot_width = tile_values.shape[3]
    sources = lax.axis_size("row")
    groups = lax.axis_size("col")
    per_piece = owned_rows // height
    inv_root = lax.rsqrt(degree.astype(jnp.float32))
    basis_wide = krylov_block.astype(jnp.float32)
    scaled = (basis_wide * inv_root[None, :]).astype(jnp.bfloat16)
    gathered = lax.all_gather(scaled, "row", axis=1, tiled=True)
    blocks = gathered.reshape(vectors, sources * per_piece, height)
    pick_index = tile_column[:, 0, :].reshape(-1)
    chosen = jnp.take(blocks, pick_index, axis=1)
    chosen = chosen * tile_live[:, 0, :].reshape(1, -1, 1).astype(jnp.bfloat16)
    chosen = chosen.reshape(vectors, block_rows, slot_width)
    panel = tile_values[:, 0]
    whole_rows = jnp.einsum("klc,luc->klu", chosen, panel, preferred_element_type=jnp.float32)
    whole_rows = whole_rows.reshape(vectors, block_rows * height)
    spread = lax.psum_scatter(whole_rows, "col", scatter_dimension=1, tiled=True)
    applied = basis_wide - inv_root[None, :] * spread
    quotient, energy = lax.psum(
        (gram_of(basis_wide, applied), gram_of(applied, applied)), ("row", "col")
    )
    factor = jnp.linalg.cholesky(energy)
    identity = jnp.eye(vectors, dtype=jnp.float32)
    inverse = lax.linalg.triangular_solve(factor, identity, left_side=True, lower=True)
    total_rows = sources * groups * owned_rows
    orthonormal = jnp.dot(inverse, applied, precision=lax.Precision.HIGHEST) * math.sqrt(total_rows)
    return (orthonormal, quotient / total_rows)


def solution(mesh):
    return jax.shard_map(
        on_device,
        mesh=mesh,
        in_specs=(
            P(None, ("row", "col")),
            P(("row", "col")),
            P("row", "col", None, None),
            P("row", "col", None),
            P("row", "col", None),
        ),
        out_specs=(P(None, ("row", "col")), P()),
        check_vma=False,
    )
```

profile of v0, /device:TPU:0, one launch (start us, length us, event | category | flops | bytes accessed | tf_op | source)
XLA Modules:
  0.0 156.6 jit_solution(8631686106743871151)
XLA Ops:
  7.2 0.0 copy-start
  7.2 0.0 reduce-scatter.2.cloned.1.call-start
  7.2 0.9 copy.22
  8.1 0.7 compare_and_fusion
  8.8 0.7 convert_rsqrt_fusion
  9.5 0.9 fusion.8
  10.4 33.0 %all_gather.3 = bf16[64,4096]{1,0:T(8,128)(2,1)S(1)} all-gather(bf16[64,512]{1,0:T(8,128)(2,1)S(1)} %fusion.8), channel_id=1, replica_groups=mesh['row'=8,'col'=4] {'row'}, dimensions={1}, use_global_device_ids=true | all-gather | bytes 589824 | tf_op jit(solution)/shard_map/all_gather | solution.py:30
  43.4 2.1 %reshape.72 = bf16[64,64,64]{2,1,0:T(8,128)(2,1)} reshape(bf16[64,4096]{1,0:T(8,128)(2,1)S(1)} %all_gather.3) | data formatting | bytes 1048576 | tf_op jit(solution)/shard_map/reshape | solution.py:31
  45.5 1.9 %copy.23 = bf16[64,64,64]{2,0,1:T(8,128)(2,1)S(1)} copy(bf16[64,64,64]{2,1,0:T(8,128)(2,1)} %reshape.72) | data formatting | bytes 1048576 | tf_op jit(solution)/shard_map/reshape | solution.py:31
  47.4 0.1 reshape_squeeze.7
  47.5 3.1 %gather_fusion = bf16[256,64,64]{2,1,0:T(8,128)(2,1)} fusion(bf16[64,64,64]{2,0,1:T(8,128)(2,1)S(1)} %copy.23, s32[1024]{0:T(1024)S(1)} %pad_clamp_fusion), kind=kCustom, calls=%fused_computation | custom fusion | bytes 4195328 | tf_op jit(solution)/shard_map/jit(_take)/gather | solution.py:33
  50.6 6.8 %copy.24 = bf16[64,256,64]{2,1,0:T(8,128)(2,1)} copy(bf16[64,256,64]{2,0,1:T(8,128)(2,1)} %bitcast.30) | data formatting | bytes 4194304 | tf_op jit(solution)/shard_map/jit(_take)/gather | solution.py:33
  57.4 0.0 copy-start.2
  57.4 6.5 %gather.7 = bf16[64,32,512]{2,1,0:T(8,128)(2,1)} reshape(bf16[64,256,64]{2,1,0:T(8,128)(2,1)} %copy.24) | data formatting | bytes 4194304 | tf_op jit(solution)/shard_map/jit(_take)/gather | solution.py:33
  63.9 0.0 copy-done.2
  63.9 0.1 copy.25
  64.0 0.1 mul.35
  64.1 0.1 mul.36
  64.2 0.1 copy.21
  64.3 0.1 broadcast_in_dim.18
  64.4 0.1 broadcast_in_dim.19
  64.5 1.8 %select_multiply_fusion = bf16[64,32,512]{2,1,0:T(8,128)(2,1)S(1)} fusion(bf16[64,32,512]{2,1,0:T(8,128)(2,1)} %gather.7, pred[32,512]{1,0:T(8,128)(4,1)S(1)} %broadcast_in_dim.19, bf16[32,512]{1,0:T(8,128)(2,1)S(1)} %mul.36), kind=kLoop, calls=%fused_computation.4 | loop fusion | flops 2097152 | bytes 4243456 | tf_op jit(solution)/shard_map/mul | solution.py:34
  66.3 0.0 copy-done
  66.3 1.4 fusion.3
  67.7 0.0 copy-start.1
  67.7 0.6 copy.27
  68.4 1.1 reshape.73
  69.5 0.0 reduce-scatter.2.cloned.1.call-update
  69.5 22.9 %reduce-scatter.2.cloned.1.call-done = f32[64,512]{1,0:T(8,128)} async-done(((f32[64,2048]{1,0:T(8,128)}), f32[64,512]{1,0:T(8,128)}) %reduce-scatter.2.cloned.1.call-update) | async-done | bytes 131088 | tf_op jit(solution)/shard_map/reduce_scatter | solution.py:39
  92.5 0.0 copy-done.1
  92.5 1.1 convolution_bitcast_fusion
  93.6 1.3 fusion.9
  94.8 40.0 %all-reduce = (f32[64,64]{0,1:T(8,128)S(1)}, f32[64,64]{0,1:T(8,128)S(1)}) all-reduce(f32[64,64]{0,1:T(8,128)S(1)} %fusion.9, f32[64,64]{0,1:T(8,128)S(1)} %convolution_bitcast_fusion), channel_id=1, replica_groups=mesh['row'=8,'col'=4] {'row','col'}, use_global_device_ids=true, to_apply=%region_1.2 | all-reduce | flops 8192 | bytes 65536 | tf_op jit(solution)/shard_map/psum | solution.py:41
  134.8 0.1 copy.29
  134.9 5.8 %cholesky.17 = f32[64,64]{1,0:T(8,128)S(1)} custom-call(f32[64,64]{1,0:T(8,128)S(1)} %fusion.16), custom_call_target="Cholesky" | custom-call | tf_op jit(solution)/shard_map/jit(cholesky)/cholesky | solution.py:44
  140.8 0.6 compare_reduce_fusion
  141.4 0.7 fusion.13
  142.1 4.9 %custom-call.6 = f32[1,64,64]{1,2,0:T(8,128)S(1)} custom-call(f32[1,64,64]{2,1,0:T(8,128)S(1)} %fusion.13), custom_call_target="InvertDiagBlocksLowerTriangular" | custom-call | tf_op jit(solution)/shard_map/triangular_solve | solution.py:46
  147.0 0.2 fusion.14
  147.3 0.7 copy.30
  148.0 1.8 %convolution_multiply_fusion = f32[64,512]{1,0:T(8,128)} fusion(f32[64,64]{1,0:T(8,128)S(1)} %fusion.14, bf16[64,512]{1,0:T(8,128)(2,1)S(1)} %copy-done.1, f32[64,512]{1,0:T(8,128)} %reduce-scatter.2.cloned.1.call-done, f32[512]{0:T(512)S(1)} %convert_rsqrt_fusion), kind=kOutput, calls=%fused_computation.6 | convolution fusion | flops 25296896 | bytes 346112 | tf_op jit(solution)/shard_map/dot_general | solution.py:48
  (6 shorter events, 0.1 us)
Async XLA Ops:
  7.2 59.1 %copy-start = (bf16[32,1,64,512]{3,2,1,0:T(8,128)(2,1)S(1)}, bf16[32,1,64,512]{3,2,1,0:T(8,128)(2,1)}, u32[]{:S(2)}) copy-start(bf16[32,1,64,512]{3,2,1,0:T(8,128)(2,1)} %param.7) | copy-start | bytes 6291460
  7.2 85.3 %reduce-scatter.2.cloned.1.call-start = ((), (), s32[]{:S(2)}) async-start(), calls=%async_computation.1 | async-start | bytes 655360 | tf_op jit(solution)/shard_map/reduce_scatter | solution.py:39
  57.4 6.5 %copy-start.2 = (s32[32,1,8]{0,2,1:T(8,128)S(1)}, s32[32,1,8]{0,2,1:T(8,128)}, u32[]{:S(2)}) copy-start(s32[32,1,8]{0,2,1:T(8,128)} %param.9) | copy-start | bytes 3076
  67.7 24.7 %copy-start.1 = (bf16[64,512]{1,0:T(8,128)(2,1)S(1)}, bf16[64,512]{1,0:T(8,128)(2,1)}, u32[]{:S(2)}) copy-start(bf16[64,512]{1,0:T(8,128)(2,1)} %param.5) | copy-start | bytes 196612
Sparse Core Ops, SparseCore 0:
  69.7 22.7 reduce-scatter.1
where the time goes:
time: 157 us
  blocking collectives  73 us (46%)
  local copies, waits for them, and re-layouts  24.5 us (16%)
  waiting for transfers between devices  22.9 us (15%)
  other arithmetic  16.1 us (10%)
  between operations  14.1 us (9%)
  matrix products  5.85 us (4%)
    psum x1, blocking collectives, on_device(): lax.psum((gram_of(basis_wide, applied), gram_of(applied, applied)), ('row...  40 us
    all_gather x1, blocking collectives, on_device(): gathered = lax.all_gather(scaled, 'row', axis=1, tiled=True)  33 us
    reduce_scatter x1, waiting for transfers between devices, on_device(): lax.psum_scatter(whole_rows, 'col', scatter_dimension=1, tiled=True)  22.9 us
    gather x3, local copies, waits for them, and re-layouts, on_device(): chosen = jnp.take(blocks, pick_index, axis=1)  16.3 us
    another operation x3, other arithmetic, on_device(): factor = jnp.linalg.cholesky(energy)  6.52 us
    another operation x2, other arithmetic, on_device(): lax.linalg.triangular_solve(factor, identity, left_side=True, lower=True)  5.55 us
    reshape x2, local copies, waits for them, and re-layouts, on_device(): blocks = gathered.reshape(vectors, sources * per_piece, height)  4.01 us
  transfers between devices with their start and end apart: 1, of which 1 were waited for; matrix products, arithmetic and copies ran while one was open for 0% of the time, Pallas kernels for 0%

commit v1 on v0

--- a/solution.py
+++ b/solution.py
@@ -3,6 +3,27 @@
 import jax.numpy as jnp
 from jax import lax
 from jax.sharding import PartitionSpec as P
+
+
+def collect(x, axis, dim):
+    size, index, rows = (lax.axis_size(axis), lax.axis_index(axis), x.shape[dim])
+    ahead = [(i, (i + 1) % size) for i in range(size)]
+    left = [(i, (i - 1) % size) for i in range(size)]
+    out = jnp.zeros((*x.shape[:dim], size * rows, *x.shape[dim + 1 :]), x.dtype)
+    out = lax.dynamic_update_slice_in_dim(out, x, index * rows, axis=dim)
+    from_left = from_right = x
+    half = size // 2
+    for step in range(1, half + 1):
+        from_left = lax.ppermute(from_left, axis, ahead)
+        out = lax.dynamic_update_slice_in_dim(
+            out, from_left, (index - step) % size * rows, axis=dim
+        )
+        if step < size - half:
+            from_right = lax.ppermute(from_right, axis, left)
+            out = lax.dynamic_update_slice_in_dim(
+                out, from_right, (index + step) % size * rows, axis=dim
+            )
+    return out
 
 
 def gram_of(left, right):
@@ -27,7 +48,7 @@
     inv_root = lax.rsqrt(degree.astype(jnp.float32))
     basis_wide = krylov_block.astype(jnp.float32)
     scaled = (basis_wide * inv_root[None, :]).astype(jnp.bfloat16)
-    gathered = lax.all_gather(scaled, "row", axis=1, tiled=True)
+    gathered = collect(scaled, "row", 1)
     blocks = gathered.reshape(vectors, sources * per_piece, height)
     pick_index = tile_column[:, 0, :].reshape(-1)
     chosen = jnp.take(blocks, pick_index, axis=1)

time: 157 us -> 148 us (0.943)
  blocking collectives: 73 us -> 40 us
  starting transfers between devices: 0.04 us -> 15.6 us
  waiting for transfers between devices: 22.9 us -> 30.6 us
    all_gather x1 -> x0, blocking collectives: 33 us -> none  [on_device(): gathered = lax.all_gather(scaled, 'row', axis=1, tiled=True)]
    ppermute x0 -> x7, starting transfers between devices: none -> 15.6 us  [the longest x3 12.5 us: collect(): from_right = lax.ppermute(from_right, axis, left)]
    ppermute x0 -> x7, waiting for transfers between devices: none -> 11.3 us  [the longest x4 11.3 us: collect(): from_left = lax.ppermute(from_left, axis, ahead)]
    reduce_scatter x1, waiting for transfers between devices: 22.9 us -> 19.3 us  [on_device(): lax.psum_scatter(whole_rows, 'col', scatter_dimension=1, tiled=True)]
  transfers between devices with their start and end apart: 1 -> 8, of which waited for: 1 -> 4; matrix products, arithmetic and copies ran while one was open for 0% -> 2% of each run, Pallas kernels for 0% -> 0%
where the time goes in v1:
time: 148 us
  blocking collectives  40 us (27%)
  waiting for transfers between devices  30.6 us (21%)
  local copies, waits for them, and re-layouts  24.5 us (17%)
  other arithmetic  17 us (11%)
  starting transfers between devices  15.6 us (11%)
  between operations  14.3 us (10%)
  matrix products  5.85 us (4%)
    psum x1, blocking collectives, on_device(): lax.psum((gram_of(basis_wide, applied), gram_of(applied, applied)), ('row...  40 us
    reduce_scatter x1, waiting for transfers between devices, on_device(): lax.psum_scatter(whole_rows, 'col', scatter_dimension=1, tiled=True)  19.3 us
    gather x3, local copies, waits for them, and re-layouts, on_device(): chosen = jnp.take(blocks, pick_index, axis=1)  16.3 us
    ppermute x3, starting transfers between devices, collect(): from_right = lax.ppermute(from_right, axis, left)  12.5 us
    ppermute x4, waiting for transfers between devices, collect(): from_left = lax.ppermute(from_left, axis, ahead)  11.3 us
    another operation x3, other arithmetic, on_device(): factor = jnp.linalg.cholesky(energy)  6.52 us
    another operation x2, other arithmetic, on_device(): lax.linalg.triangular_solve(factor, identity, left_side=True, lower=True)  5.55 us
    reshape x2, local copies, waits for them, and re-layouts, on_device(): blocks = gathered.reshape(vectors, sources * per_piece, height)  3.99 us
  transfers between devices with their start and end apart: 8, of which 4 were waited for; matrix products, arithmetic and copies ran while one was open for 2% of the time, Pallas kernels for 0%

profile of v1, /device:TPU:0, one launch (start us, length us, event | category | flops | bytes accessed | tf_op | source)
XLA Modules:
  0.0 147.8 jit_solution(4958539220924424243)
XLA Ops:
  7.2 0.0 copy-start
  7.2 0.0 reduce-scatter.2.cloned.1.call-start
  7.2 0.8 convert_rsqrt_fusion
  8.1 0.9 constant_dynamic-update-slice_fusion.7
  9.0 3.0 %collective-permute-start = (bf16[64,512]{1,0:T(8,128)(2,1)S(1)}, bf16[64,512]{1,0:T(8,128)(2,1)S(1)}, u32[]{:S(2)}, u32[]{:S(2)}) collective-permute-start(bf16[64,512]{1,0:T(8,128)(2,1)S(1)} %get-tuple-element.11), channel_id=1, source_target_pairs={{0,4},{4,8},{8,12},{12,16},{16,20},{20,24},{24,28},{28,0},{1,5},{5... | collective-permute-start | bytes 196616 | tf_op jit(solution)/shard_map/ppermute | solution.py:17
  12.0 3.1 %collective-permute-start.1 = (bf16[64,512]{1,0:T(8,128)(2,1)S(1)}, bf16[64,512]{1,0:T(8,128)(2,1)S(1)}, u32[]{:S(2)}, u32[]{:S(2)}) collective-permute-start(bf16[64,512]{1,0:T(8,128)(2,1)S(1)} %get-tuple-element.11), channel_id=1, source_target_pairs={{0,28},{4,0},{8,4},{12,8},{16,12},{20,16},{24,20},{28,24},{1,29},{... | collective-permute-start | bytes 196616 | tf_op jit(solution)/shard_map/ppermute | solution.py:22
  15.1 0.8 copy.22
  15.8 0.7 compare_and_fusion
  16.5 0.1 reshape_squeeze.7
  16.6 0.7 convert_bitcast_fusion
  17.3 0.1 copy.25
  17.4 0.1 mul.67
  17.5 0.1 mul.68
  17.6 0.1 copy.21
  17.7 0.1 broadcast_in_dim.21
  17.8 0.1 broadcast_in_dim.22
  18.0 0.0 collective-permute-done
  18.0 0.1 collective-permute-start.2
  18.1 0.0 collective-permute-done.1
  18.1 4.7 %collective-permute-start.3 = (bf16[64,512]{1,0:T(8,128)(2,1)S(1)}, bf16[64,512]{1,0:T(8,128)(2,1)S(1)}, u32[]{:S(2)}, u32[]{:S(2)}) collective-permute-start(bf16[64,512]{1,0:T(8,128)(2,1)S(1)} %collective-permute-done.1), channel_id=1, source_target_pairs={{0,28},{4,0},{8,4},{12,8},{16,12},{20,16},{24,20},{28,24},{1,29},{... | collective-permute-start | bytes 196616 | tf_op jit(solution)/shard_map/ppermute | solution.py:22
  22.8 2.2 %collective-permute-done.2 = bf16[64,512]{1,0:T(8,128)(2,1)S(1)} collective-permute-done((bf16[64,512]{1,0:T(8,128)(2,1)S(1)}, bf16[64,512]{1,0:T(8,128)(2,1)S(1)}, u32[]{:S(2)}, u32[]{:S(2)}) %collective-permute-start.2) | collective-permute-done | bytes 65568 | tf_op jit(solution)/shard_map/ppermute | solution.py:17
  25.0 0.0 collective-permute-start.4
  25.0 0.0 collective-permute-done.3
  25.0 4.7 %collective-permute-start.5 = (bf16[64,512]{1,0:T(8,128)(2,1)S(1)}, bf16[64,512]{1,0:T(8,128)(2,1)S(1)}, u32[]{:S(2)}, u32[]{:S(2)}) collective-permute-start(bf16[64,512]{1,0:T(8,128)(2,1)S(1)} %collective-permute-done.3), channel_id=1, source_target_pairs={{0,28},{4,0},{8,4},{12,8},{16,12},{20,16},{24,20},{28,24},{1,29},{... | collective-permute-start | bytes 196616 | tf_op jit(solution)/shard_map/ppermute | solution.py:22
  29.8 2.2 %collective-permute-done.4 = bf16[64,512]{1,0:T(8,128)(2,1)S(1)} collective-permute-done((bf16[64,512]{1,0:T(8,128)(2,1)S(1)}, bf16[64,512]{1,0:T(8,128)(2,1)S(1)}, u32[]{:S(2)}, u32[]{:S(2)}) %collective-permute-start.4) | collective-permute-done | bytes 65568 | tf_op jit(solution)/shard_map/ppermute | solution.py:17
  32.0 0.0 collective-permute-start.6
  32.0 0.0 collective-permute-done.5
  32.0 6.9 %collective-permute-done.6 = bf16[64,512]{1,0:T(8,128)(2,1)S(1)} collective-permute-done((bf16[64,512]{1,0:T(8,128)(2,1)S(1)}, bf16[64,512]{1,0:T(8,128)(2,1)S(1)}, u32[]{:S(2)}, u32[]{:S(2)}) %collective-permute-start.6) | collective-permute-done | bytes 65568 | tf_op jit(solution)/shard_map/ppermute | solution.py:17
  39.0 2.1 %reshape.72 = bf16[64,64,64]{2,1,0:T(8,128)(2,1)} reshape(bf16[64,4096]{1,0:T(8,128)(2,1)S(1)} %constant_dynamic-update-slice_fusion) | data formatting | bytes 1048576 | tf_op jit(solution)/shard_map/reshape | solution.py:52
  41.0 1.9 %copy.23 = bf16[64,64,64]{2,0,1:T(8,128)(2,1)S(1)} copy(bf16[64,64,64]{2,1,0:T(8,128)(2,1)} %reshape.72) | data formatting | bytes 1048576 | tf_op jit(solution)/shard_map/reshape | solution.py:52
  43.0 3.1 %gather_fusion = bf16[256,64,64]{2,1,0:T(8,128)(2,1)} fusion(bf16[64,64,64]{2,0,1:T(8,128)(2,1)S(1)} %copy.23, s32[1024]{0:T(1024)S(1)} %pad_clamp_fusion), kind=kCustom, calls=%fused_computation | custom fusion | bytes 4195328 | tf_op jit(solution)/shard_map/jit(_take)/gather | solution.py:54
  46.0 6.8 %copy.24 = bf16[64,256,64]{2,1,0:T(8,128)(2,1)} copy(bf16[64,256,64]{2,0,1:T(8,128)(2,1)} %bitcast.30) | data formatting | bytes 4194304 | tf_op jit(solution)/shard_map/jit(_take)/gather | solution.py:54
  52.8 6.4 %gather.7 = bf16[64,32,512]{2,1,0:T(8,128)(2,1)} reshape(bf16[64,256,64]{2,1,0:T(8,128)(2,1)} %copy.24) | data formatting | bytes 4194304 | tf_op jit(solution)/shard_map/jit(_take)/gather | solution.py:54
  59.3 1.8 %select_multiply_fusion = bf16[64,32,512]{2,1,0:T(8,128)(2,1)S(1)} fusion(bf16[64,32,512]{2,1,0:T(8,128)(2,1)} %gather.7, pred[32,512]{1,0:T(8,128)(4,1)S(1)} %broadcast_in_dim.22, bf16[32,512]{1,0:T(8,128)(2,1)S(1)} %mul.68), kind=kLoop, calls=%fused_computation.4 | loop fusion | flops 2097152 | bytes 4243456 | tf_op jit(solution)/shard_map/mul | solution.py:55
  61.1 0.0 copy-done
  61.1 1.4 fusion.3
  62.5 0.0 copy-start.1
  62.5 0.6 copy.27
  63.1 1.2 reshape.73
  64.3 0.0 reduce-scatter.2.cloned.1.call-update
  64.3 19.3 %reduce-scatter.2.cloned.1.call-done = f32[64,512]{1,0:T(8,128)} async-done(((f32[64,2048]{1,0:T(8,128)}), f32[64,512]{1,0:T(8,128)}) %reduce-scatter.2.cloned.1.call-update) | async-done | bytes 131088 | tf_op jit(solution)/shard_map/reduce_scatter | solution.py:60
  83.6 0.0 copy-done.1
  83.6 1.1 convolution_bitcast_fusion
  84.7 1.3 fusion.9
  85.9 40.0 %all-reduce = (f32[64,64]{0,1:T(8,128)S(1)}, f32[64,64]{0,1:T(8,128)S(1)}) all-reduce(f32[64,64]{0,1:T(8,128)S(1)} %fusion.9, f32[64,64]{0,1:T(8,128)S(1)} %convolution_bitcast_fusion), channel_id=1, replica_groups=mesh['row'=8,'col'=4] {'row','col'}, use_global_device_ids=true, to_apply=%region_1.2 | all-reduce | flops 8192 | bytes 65536 | tf_op jit(solution)/shard_map/psum | solution.py:62
  126.0 0.1 copy.29
  126.1 5.8 %cholesky.17 = f32[64,64]{1,0:T(8,128)S(1)} custom-call(f32[64,64]{1,0:T(8,128)S(1)} %fusion.16), custom_call_target="Cholesky" | custom-call | tf_op jit(solution)/shard_map/jit(cholesky)/cholesky | solution.py:65
  131.9 0.6 compare_reduce_fusion
  132.6 0.7 fusion.13
  133.2 4.9 %custom-call.6 = f32[1,64,64]{1,2,0:T(8,128)S(1)} custom-call(f32[1,64,64]{2,1,0:T(8,128)S(1)} %fusion.13), custom_call_target="InvertDiagBlocksLowerTriangular" | custom-call | tf_op jit(solution)/shard_map/triangular_solve | solution.py:67
  138.1 0.2 fusion.14
  138.4 0.7 copy.30
  139.1 1.8 %convolution_multiply_fusion = f32[64,512]{1,0:T(8,128)} fusion(f32[64,64]{1,0:T(8,128)S(1)} %fusion.14, bf16[64,512]{1,0:T(8,128)(2,1)S(1)} %copy-done.1, f32[64,512]{1,0:T(8,128)} %reduce-scatter.2.cloned.1.call-done, f32[512]{0:T(512)S(1)} %convert_rsqrt_fusion), kind=kOutput, calls=%fused_computation.6 | convolution fusion | flops 25296896 | bytes 346112 | tf_op jit(solution)/shard_map/dot_general | solution.py:69
  (13 shorter events, 0.2 us)
Async XLA Ops:
  7.2 53.9 %copy-start = (bf16[32,1,64,512]{3,2,1,0:T(8,128)(2,1)S(1)}, bf16[32,1,64,512]{3,2,1,0:T(8,128)(2,1)}, u32[]{:S(2)}) copy-start(bf16[32,1,64,512]{3,2,1,0:T(8,128)(2,1)} %param.7) | copy-start | bytes 6291460
  7.2 76.4 %reduce-scatter.2.cloned.1.call-start = ((), (), s32[]{:S(2)}) async-start(), calls=%async_computation.1 | async-start | bytes 655360 | tf_op jit(solution)/shard_map/reduce_scatter | solution.py:60
  9.0 9.0 %collective-permute-start = (bf16[64,512]{1,0:T(8,128)(2,1)S(1)}, bf16[64,512]{1,0:T(8,128)(2,1)S(1)}, u32[]{:S(2)}, u32[]{:S(2)}) collective-permute-start(bf16[64,512]{1,0:T(8,128)(2,1)S(1)} %get-tuple-element.11), channel_id=1, source_target_pairs={{0,4},{4,8},{8,12},{12,16},{16,20},{20,24},{24,28},{28,0},{1,5},{5... | collective-permute-start | bytes 196616 | tf_op jit(solution)/shard_map/ppermute | solution.py:17
  12.0 6.1 %collective-permute-start.1 = (bf16[64,512]{1,0:T(8,128)(2,1)S(1)}, bf16[64,512]{1,0:T(8,128)(2,1)S(1)}, u32[]{:S(2)}, u32[]{:S(2)}) collective-permute-start(bf16[64,512]{1,0:T(8,128)(2,1)S(1)} %get-tuple-element.11), channel_id=1, source_target_pairs={{0,28},{4,0},{8,4},{12,8},{16,12},{20,16},{24,20},{28,24},{1,29},{... | collective-permute-start | bytes 196616 | tf_op jit(solution)/shard_map/ppermute | solution.py:22
  18.0 7.0 %collective-permute-start.2 = (bf16[64,512]{1,0:T(8,128)(2,1)S(1)}, bf16[64,512]{1,0:T(8,128)(2,1)S(1)}, u32[]{:S(2)}, u32[]{:S(2)}) collective-permute-start(bf16[64,512]{1,0:T(8,128)(2,1)S(1)} %collective-permute-done), channel_id=1, source_target_pairs={{0,4},{4,8},{8,12},{12,16},{16,20},{20,24},{24,28},{28,0},{1,5},{5... | collective-permute-start | bytes 196616 | tf_op jit(solution)/shard_map/ppermute | solution.py:17
  18.1 6.9 %collective-permute-start.3 = (bf16[64,512]{1,0:T(8,128)(2,1)S(1)}, bf16[64,512]{1,0:T(8,128)(2,1)S(1)}, u32[]{:S(2)}, u32[]{:S(2)}) collective-permute-start(bf16[64,512]{1,0:T(8,128)(2,1)S(1)} %collective-permute-done.1), channel_id=1, source_target_pairs={{0,28},{4,0},{8,4},{12,8},{16,12},{20,16},{24,20},{28,24},{1,29},{... | collective-permute-start | bytes 196616 | tf_op jit(solution)/shard_map/ppermute | solution.py:22
  25.0 7.0 %collective-permute-start.4 = (bf16[64,512]{1,0:T(8,128)(2,1)S(1)}, bf16[64,512]{1,0:T(8,128)(2,1)S(1)}, u32[]{:S(2)}, u32[]{:S(2)}) collective-permute-start(bf16[64,512]{1,0:T(8,128)(2,1)S(1)} %collective-permute-done.2), channel_id=1, source_target_pairs={{0,4},{4,8},{8,12},{12,16},{16,20},{20,24},{24,28},{28,0},{1,5},{5... | collective-permute-start | bytes 196616 | tf_op jit(solution)/shard_map/ppermute | solution.py:17
  25.0 7.0 %collective-permute-start.5 = (bf16[64,512]{1,0:T(8,128)(2,1)S(1)}, bf16[64,512]{1,0:T(8,128)(2,1)S(1)}, u32[]{:S(2)}, u32[]{:S(2)}) collective-permute-start(bf16[64,512]{1,0:T(8,128)(2,1)S(1)} %collective-permute-done.3), channel_id=1, source_target_pairs={{0,28},{4,0},{8,4},{12,8},{16,12},{20,16},{24,20},{28,24},{1,29},{... | collective-permute-start | bytes 196616 | tf_op jit(solution)/shard_map/ppermute | solution.py:22
  32.0 7.0 %collective-permute-start.6 = (bf16[64,512]{1,0:T(8,128)(2,1)S(1)}, bf16[64,512]{1,0:T(8,128)(2,1)S(1)}, u32[]{:S(2)}, u32[]{:S(2)}) collective-permute-start(bf16[64,512]{1,0:T(8,128)(2,1)S(1)} %collective-permute-done.4), channel_id=1, source_target_pairs={{0,4},{4,8},{8,12},{12,16},{16,20},{20,24},{24,28},{28,0},{1,5},{5... | collective-permute-start | bytes 196616 | tf_op jit(solution)/shard_map/ppermute | solution.py:17
  62.5 21.1 %copy-start.1 = (bf16[64,512]{1,0:T(8,128)(2,1)S(1)}, bf16[64,512]{1,0:T(8,128)(2,1)}, u32[]{:S(2)}) copy-start(bf16[64,512]{1,0:T(8,128)(2,1)} %param.5) | copy-start | bytes 196612
Sparse Core Ops, SparseCore 0:
  64.4 19.0 reduce-scatter.1
